TPU v7x, 32 devices: a whole 2x2x4 slice. The times are simulated.
32 devices in a mesh: lon: 8 (over z, core), mem: 4 (over y, x).
Axes of the slice: x: 2, y: 2, z: 4, core: 2. Of those that a mesh axis runs over, the one named last changes fastest.
Arguments:
- members: float32 [32, 4, 192, 256], P('mem', None, 'lon'), may hold values from -6 to 6
- courant_lon: float32 [4, 192, 256], P(None, 'lon'), may hold values from -0.55 to 0.55
- courant_lat: float32 [4, 192, 256], P(None, 'lon'), may hold values from -0.4 to 0.4
- vert_modes: float32 [2, 4], replicated, may hold values from -1 to 1
- horiz_modes: float32 [4, 192, 256], P(None, 'lon'), may hold values from -1 to 1
- obs_index: int32 [16384], P('lon'), may hold values from 0 to 24575
- obs_count: int32 [8], P('lon'), may hold values from 1024 to 2048, as said below
- obs_value: float32 [16384], P('lon'), may hold values from -6 to 6
- obs_var: float32 [16384], P('lon'), may hold values from 2 to 48
Outputs:
- prior_trajectories: float32 [32, 4, 192, 256], P('mem', None, 'lon')
- analysis_mean: float32 [4, 192, 256], P(None, 'lon')
Inputs may be any that keep to these rules, and one draw needn't show every extreme that they name: `obs_index`: index of a cell within the band's own block: level, then longitude within the band, then latitude. Each band uses its first obs_count slots; some band uses all 2048.
All inputs are finite; a program needn't handle non-finite values.
Results may differ from a plain program's by a relative error of at most 0.0001.
Values sent between devices are 32-bit elements; how exact they have to be, the bound alone decides.
A program may use at most 128 MiB of HBM per device.

v0:
```python
import jax
import jax.numpy as jnp
from jax import lax
from jax.sharding import PartitionSpec as P

KV = 2
KH = 4
ADV_STEPS = 2


def padded(block, sides, width):
    for axis, dim in sides:
        count = lax.axis_size(axis)
        forward = [(i, i + 1) for i in range(count - 1)]
        forward.append((count - 1, 0))
        backward = [(target, source) for source, target in forward]
        low = lax.ppermute(
            lax.slice_in_dim(block, block.shape[dim] - width, None, axis=dim), axis, forward
        )
        high = lax.ppermute(lax.slice_in_dim(block, 0, width, axis=dim), axis, backward)
        block = jnp.concatenate([low, block, high], axis=dim)
    return block


def update(centre, western, eastern, flow_lon, flow_lat):
    zero_col = jnp.zeros_like(centre[..., :1])
    south_boundary = jnp.concatenate([zero_col, centre[..., :-1]], axis=-1)
    northern = jnp.concatenate([centre[..., 1:], zero_col], axis=-1)
    result = centre - jnp.maximum(flow_lon, 0.0) * (centre - western)
    result = result - jnp.minimum(flow_lon, 0.0) * (eastern - centre)
    result = result - jnp.maximum(flow_lat, 0.0) * (centre - south_boundary)
    result = result - jnp.minimum(flow_lat, 0.0) * (northern - centre)
    return result


def per_device(
    members,
    courant_lon,
    courant_lat,
    vert_modes,
    horiz_modes,
    obs_index,
    obs_count,
    obs_value,
    obs_var,
):
    mem_dev, layer_tally, band_width, lat_rows = members.shape
    sample_tally_overall = mem_dev * lax.axis_size("mem")
    rim_depth = ADV_STEPS
    stacked = jnp.concatenate(
        [members.reshape(mem_dev * layer_tally, band_width, lat_rows), courant_lon, courant_lat],
        axis=0,
    )
    extended = padded(stacked, (("lon", 1),), rim_depth)
    split_at = mem_dev * layer_tally
    prognostic_vector = extended[:split_at].reshape(
        mem_dev, layer_tally, band_width + 2 * rim_depth, lat_rows
    )
    flow_lon_ext = extended[split_at : split_at + layer_tally]
    meridional_wind_padded = extended[split_at + layer_tally :]
    for section in range(rim_depth):
        out_cols = band_width + 2 * (rim_depth - 1 - section)
        first_col = section + 1
        prognostic_vector = update(
            prognostic_vector[:, :, 1 : out_cols + 1],
            prognostic_vector[:, :, 0:out_cols],
            prognostic_vector[:, :, 2 : out_cols + 2],
            flow_lon_ext[:, first_col : first_col + out_cols],
            meridional_wind_padded[:, first_col : first_col + out_cols],
        )
    sample_centroid = lax.psum(jnp.sum(prognostic_vector, axis=0), "mem") / sample_tally_overall
    sample_departure = prognostic_vector - sample_centroid[None]
    norm_scale = (sample_tally_overall - 1) ** (-0.5)
    obs_slots = obs_index.shape[0]
    band_cells = band_width * lat_rows
    level_idx = obs_index // band_cells
    within = obs_index % band_cells
    anomaly_obs = jnp.take(sample_departure.reshape(mem_dev, -1), obs_index, axis=1)
    mean_obs = jnp.take(sample_centroid.reshape(-1), obs_index)
    vert_obs = jnp.take(vert_modes, level_idx, axis=1)
    horiz_obs = jnp.take(horiz_modes.reshape(KH, -1), within, axis=1)
    modes_obs = (vert_obs[:, None, :] * horiz_obs[None, :, :]).reshape(KV * KH, obs_slots)
    live_mask = (jnp.arange(obs_slots, dtype=jnp.int32) < obs_count[0]).astype(jnp.float32)
    obs_perts = (
        anomaly_obs[:, None, :] * modes_obs[None, :, :] * (live_mask * norm_scale)[None, None, :]
    )
    obs_perts = obs_perts.reshape(mem_dev * KV * KH, obs_slots)
    inv_var = live_mask / obs_var
    innovation = obs_value - mean_obs
    all_perts = lax.all_gather(obs_perts, "mem", axis=0, tiled=True)
    gram_part = jnp.dot(all_perts * inv_var[None, :], all_perts.T, precision=lax.Precision.HIGHEST)
    side_part = jnp.dot(all_perts, inv_var * innovation, precision=lax.Precision.HIGHEST)
    gram_matrix, right_side = lax.psum((gram_part, side_part), "lon")
    system = jnp.eye(gram_matrix.shape[0], dtype=jnp.float32) + gram_matrix
    factor = jnp.linalg.cholesky(system)
    weights = jax.scipy.linalg.cho_solve((factor, True), right_side)
    w_mat = weights.reshape(sample_tally_overall, KV * KH)
    w_local = lax.dynamic_slice_in_dim(w_mat, lax.axis_index("mem") * mem_dev, mem_dev, 0)
    mode_coef = jnp.einsum(
        "mk,mlij->klij", w_local, sample_departure, precision=lax.Precision.HIGHEST
    )
    mode_coef = mode_coef.reshape(KV, KH, layer_tally, band_width, lat_rows)
    inc_part = (
        jnp.einsum(
            "al,bij,ablij->lij", vert_modes, horiz_modes, mode_coef, precision=lax.Precision.HIGHEST
        )
        * norm_scale
    )
    posterior_adjustment = lax.psum(inc_part, "mem")
    return (prognostic_vector, sample_centroid + posterior_adjustment)


def solution(mesh):
    placed = (
        P("mem", None, "lon", None),
        P(None, "lon", None),
        P(None, "lon", None),
        P(),
        P(None, "lon", None),
        P("lon"),
        P("lon"),
        P("lon"),
        P("lon"),
    )
    return jax.shard_map(
        per_device,
        mesh=mesh,
        in_specs=placed,
        out_specs=(P("mem", None, "lon", None), P(None, "lon", None)),
        check_vma=False,
    )
```

profile of v0, /device:TPU:0, one launch (start us, length us, event | category | flops | bytes accessed | tf_op | source)
XLA Modules:
  0.0 332.7 jit_solution(16638624239704680310)
XLA Ops:
  7.2 1.2 pad_maximum_fusion.5
  8.4 0.5 collective-permute-start
  8.9 4.1 %collective-permute-start.1 = (f32[40,2,256]{2,1,0:T(2,128)S(1)}, f32[40,2,256]{2,1,0:T(2,128)S(1)}, u32[]{:S(2)}, u32[]{:S(2)}) collective-permute-start(f32[40,2,256]{2,1,0:T(2,128)S(1)} %get-tuple-element.36), channel_id=1, source_target_pairs={{4,0},{8,4},{12,8},{16,12},{20,16},{24,20},{28,24},{0,28},{5,1},{9... | collective-permute-start | bytes 245768 | tf_op jit(solution)/shard_map/ppermute | solution.py:20
  13.0 0.7 compare_and_fusion.1
  13.8 0.7 fusion.30
  14.5 0.8 copy.32
  15.2 5.5 %gather_fusion.1 = f32[2048,2]{1,0:T(8,128)S(1)} fusion(f32[2,4]{0,1:T(4,128)S(1)} %copy.32, s32[2048]{0:T(1024)S(1)} %get-tuple-element.46), kind=kCustom, calls=%fused_computation.1 | custom fusion | bytes 40960 | tf_op jit(solution)/shard_map/jit(_take)/gather | solution.py:80
  20.7 0.3 select_bitcast_fusion.1
  21.0 0.3 copy.33
  21.4 2.3 copy.34
  23.6 7.4 %gather_fusion.2 = f32[2048,4]{1,0:T(8,128)S(1)} fusion(f32[4,6144]{0,1:T(8,128)} %bitcast.119, s32[2048]{0:T(1024)S(1)} %get-tuple-element.47), kind=kCustom, calls=%fused_computation.2 | custom fusion | bytes 73728 | tf_op jit(solution)/shard_map/jit(_take)/gather | solution.py:81
  31.1 0.3 select_bitcast_fusion
  31.4 0.3 copy.35
  32.9 0.4 fusion.43
  33.4 0.7 fusion.9
  34.1 0.3 fusion.42
  34.4 1.2 fusion.39
  35.6 41.8 %all-reduce.9.cloned.1.call-done = f32[4,24,256]{2,1,0:T(8,128)} async-done(((f32[4,24,256]{2,1,0:T(8,128)}), f32[4,24,256]{2,1,0:T(8,128)}) %all-reduce.9.cloned.1.call-update) | async-done | bytes 98320 | tf_op jit(solution)/shard_map/psum | solution.py:71
  77.5 0.9 broadcast_multiply_fusion
  78.5 6.6 %copy.30 = f32[8,4,24,256]{0,3,2,1:T(8,128)} copy(f32[8,4,24,256]{3,2,1,0:T(8,128)S(1)} %broadcast_subtract_fusion) | data formatting | bytes 1572864 | tf_op jit(solution)/shard_map/sub | solution.py:72
  85.1 11.8 %gather_fusion.3 = f32[2048]{0:T(1024)S(1)} fusion(f32[24576]{0:T(1024)S(1)} %bitcast.112, s32[2048]{0:T(1024)S(1)} %get-tuple-element.45), kind=kCustom, calls=%fused_computation.3 | custom fusion | bytes 24576 | tf_op jit(solution)/shard_map/jit(_take)/gather | solution.py:79
  96.9 10.0 %gather_fusion = f32[2048,8]{1,0:T(8,128)S(1)} fusion(f32[8,24576]{0,1:T(8,128)} %bitcast.113, s32[2048]{0:T(1024)S(1)} %get-tuple-element.45), kind=kCustom, calls=%fused_computation | custom fusion | bytes 139264 | tf_op jit(solution)/shard_map/jit(_take)/gather | solution.py:78
  107.0 0.3 select_bitcast_fusion.2
  107.6 0.9 bitcast_multiply_fusion
  108.8 35.2 %all-gather.2.cloned.1.call-done = f32[256,2048]{1,0:T(8,128)} async-done(((f32[64,2048]{1,0:T(8,128)}), f32[256,2048]{1,0:T(8,128)}) %all-gather.2.cloned.1.call-update) | async-done | bytes 2097168 | tf_op jit(solution)/shard_map/all_gather | solution.py:90
  144.0 5.0 %fusion = f32[256,256]{0,1:T(8,128)} fusion(f32[256,2048]{1,0:T(8,128)} %all-gather.2.cloned.1.call-done, f32[2048]{0:T(1024)S(1)} %get-tuple-element.19), kind=kOutput, calls=%fused_computation.6 | convolution fusion | flops 1611137024 | bytes 2367488 | tf_op jit(solution)/shard_map/dot_general | solution.py:91
  149.1 1.7 fusion.44
  150.8 16.6 %psum.30 = f32[256]{0:T(256)S(1)} all-reduce(f32[256]{0:T(256)S(1)} %bitcast.124), channel_id=1, replica_groups=mesh['lon'=8,'mem'=4] {'lon'}, use_global_device_ids=true, to_apply=%region_7.8 | all-reduce | flops 256 | bytes 2048 | tf_op jit(solution)/shard_map/psum | solution.py:93
  167.4 36.7 %all-reduce.11.cloned.1.call-done = f32[256,256]{0,1:T(8,128)} async-done(((f32[256,256]{0,1:T(8,128)}), f32[256,256]{0,1:T(8,128)}) %all-reduce.11.cloned.1.call-update) | async-done | bytes 262160 | tf_op jit(solution)/shard_map/psum | solution.py:93
  204.1 1.0 convert_add_fusion
  205.2 1.0 fusion.19
  206.2 11.7 %cholesky.50 = f32[128,128]{1,0:T(8,128)S(1)} custom-call(f32[128,128]{1,0:T(8,128)S(1)} %cholesky.118), custom_call_target="Cholesky" | custom-call | tf_op jit(solution)/shard_map/jit(cholesky)/cholesky | solution.py:95
  218.0 0.7 compare_reduce_fusion.1
  218.7 9.8 %custom-call.18 = f32[1,128,128]{1,2,0:T(8,128)S(1)} custom-call(f32[1,128,128]{2,1,0:T(8,128)S(1)} %get-tuple-element.44), custom_call_target="InvertDiagBlocksLowerTriangular" | custom-call | tf_op jit(solution)/shard_map/jit(cholesky)/cholesky | solution.py:95
  229.0 11.7 %cholesky.105 = f32[128,128]{1,0:T(8,128)S(1)} custom-call(f32[128,128]{1,0:T(8,128)S(1)} %convolution_subtract_fusion), custom_call_target="Cholesky" | custom-call | tf_op jit(solution)/shard_map/jit(cholesky)/cholesky | solution.py:95
  240.7 0.6 compare_reduce_fusion
  242.6 3.8 %while.1 = (s32[]{:T(128)}, f32[256,256]{1,0:T(8,128)S(1)}, s32[2,2]{1,0:T(2,128)S(1)}, f32[2,128,128]{2,1,0:T(8,128)S(1)}, s32[]{:T(128)}) while((s32[]{:T(128)}, f32[256,256]{1,0:T(8,128)S(1)}, s32[2,2]{1,0:T(2,128)S(1)}, f32[2,128,128]{2,1,0:T(8,128)S(1)}, s32[]{:T(128)}) %tuple.44), condition=%wide.while_cond, body=%wide.while_body.sunk | while | flops 2 | bytes 131189 | solution.py:96
  242.6 0.6 fusion.57
  243.2 1.3 bitcast_dynamic-update-slice_fusion.2
  244.5 0.6 fusion.57
  245.2 1.3 bitcast_dynamic-update-slice_fusion.2
  246.4 19.9 %custom-call.19 = f32[2,128,128]{1,2,0:T(8,128)S(1)} custom-call(f32[2,128,128]{2,1,0:T(8,128)S(1)} %get-tuple-element.9), custom_call_target="InvertDiagBlocksLowerTriangular" | custom-call | tf_op jit(solution)/shard_map/jit(_cho_solve)/triangular_solve | solution.py:96
  267.6 13.6 %fusion.31 = f32[8,4,24,256]{3,0,2,1:T(8,128)S(1)} fusion(f32[8,4,24,256]{0,3,2,1:T(8,128)} %copy.30, f32[32,8]{1,0:T(8,128)S(1)} %reshape.169, s32[]{:T(128)S(6)} %select_n.71), kind=kOutput, calls=%fused_computation.98 | convolution fusion | flops 18874368 | bytes 1576964 | tf_op jit(solution)/shard_map/mk,mlij->klij/dot_general | solution.py:99
  281.5 0.6 multiply_reduce_fusion
  282.1 0.8 fusion.20
  283.0 0.7 bitcast_multiply_fusion.1
  283.6 41.0 %all-reduce.13.cloned.1.call-done = f32[4,24,256]{2,1,0:T(8,128)} async-done(((f32[4,24,256]{2,1,0:T(8,128)}), f32[4,24,256]{2,1,0:T(8,128)}) %all-reduce.13.cloned.1.call-update) | async-done | bytes 98320 | tf_op jit(solution)/shard_map/psum | solution.py:109
  324.6 1.5 fusion.38
  (69 shorter events, 3.6 us)
Async XLA Ops:
  7.2 70.3 %all-reduce.9.cloned.1.call-start = ((), (), s32[]{:S(2)}) async-start(), calls=%async_computation | async-start | bytes 196608 | tf_op jit(solution)/shard_map/psum | solution.py:71
  7.2 14.2 %copy-start.5 = (f32[4,24,256]{2,1,0:T(8,128)S(1)}, f32[4,24,256]{2,1,0:T(8,128)}, u32[]{:S(2)}) copy-start(f32[4,24,256]{2,1,0:T(8,128)} %param.13) | copy-start | bytes 294916
  8.4 24.1 %collective-permute-start = (f32[40,2,256]{2,1,0:T(2,128)S(1)}, f32[40,2,256]{2,1,0:T(2,128)S(1)}, u32[]{:S(2)}, u32[]{:S(2)}) collective-permute-start(f32[40,2,256]{2,1,0:T(2,128)S(1)} %get-tuple-element.35), channel_id=1, source_target_pairs={{0,4},{4,8},{8,12},{12,16},{16,20},{20,24},{24,28},{28,0},{1,5},{5... | collective-permute-start | bytes 245768 | tf_op jit(solution)/shard_map/ppermute | solution.py:17
  8.9 23.6 %collective-permute-start.1 = (f32[40,2,256]{2,1,0:T(2,128)S(1)}, f32[40,2,256]{2,1,0:T(2,128)S(1)}, u32[]{:S(2)}, u32[]{:S(2)}) collective-permute-start(f32[40,2,256]{2,1,0:T(2,128)S(1)} %get-tuple-element.36), channel_id=1, source_target_pairs={{4,0},{8,4},{12,8},{16,12},{20,16},{24,20},{28,24},{0,28},{5,1},{9... | collective-permute-start | bytes 245768 | tf_op jit(solution)/shard_map/ppermute | solution.py:20
  23.6 8.2 %copy-start.3 = (f32[4,24,256]{2,1,0:T(8,128)S(1)}, f32[4,24,256]{2,1,0:T(8,128)}, u32[]{:S(2)}) copy-start(f32[4,24,256]{2,1,0:T(8,128)} %param.11) | copy-start | bytes 294916
  23.6 8.2 %copy-start.4 = (f32[4,24,256]{2,1,0:T(8,128)S(1)}, f32[4,24,256]{2,1,0:T(8,128)}, u32[]{:S(2)}) copy-start(f32[4,24,256]{2,1,0:T(8,128)} %param.10) | copy-start | bytes 294916
  23.6 8.9 %copy-start.1 = (f32[8,4,24,256]{3,2,1,0:T(8,128)S(1)}, f32[8,4,24,256]{3,2,1,0:T(8,128)}, u32[]{:S(2)}) copy-start(f32[8,4,24,256]{3,2,1,0:T(8,128)} %param.9) | copy-start | bytes 2359300
  35.6 49.5 %copy-start.2 = (f32[8,4,24,256]{3,2,1,0:T(8,128)}, f32[8,4,24,256]{3,2,1,0:T(8,128)S(1)}, u32[]{:S(2)}) copy-start(f32[8,4,24,256]{3,2,1,0:T(8,128)S(1)} %get-tuple-element.22) | copy-start | bytes 2359300
  35.6 108.4 %all-gather.2.cloned.1.call-start = ((), (), s32[]{:S(2)}) async-start(), calls=%async_computation.1 | async-start | bytes 2621440 | tf_op jit(solution)/shard_map/all_gather | solution.py:90
  85.1 21.9 %copy-start.7 = (s32[2048]{0:T(1024)S(1)}, s32[2048]{0:T(1024)}, u32[]{:S(2)}) copy-start(s32[2048]{0:T(1024)} %param.14) | copy-start | bytes 24580
  85.1 21.9 %copy-start.8 = (f32[2048]{0:T(1024)S(1)}, f32[2048]{0:T(1024)}, u32[]{:S(2)}) copy-start(f32[2048]{0:T(1024)} %param.16) | copy-start | bytes 24580
  85.1 21.9 %copy-start.9 = (f32[2048]{0:T(1024)S(1)}, f32[2048]{0:T(1024)}, u32[]{:S(2)}) copy-start(f32[2048]{0:T(1024)} %param.17) | copy-start | bytes 24580
  107.0 1.6 copy-start.10
  108.5 95.6 %all-reduce.11.cloned.1.call-start = ((), (), s32[]{:S(2)}) async-start(), calls=%async_computation.2 | async-start | bytes 524288 | tf_op jit(solution)/shard_map/psum | solution.py:93
  144.0 5.1 %copy-start = (f32[256,2048]{1,0:T(8,128)S(1)}, f32[256,2048]{1,0:T(8,128)}, u32[]{:S(2)}) copy-start(f32[256,2048]{1,0:T(8,128)} %all-gather.2.cloned.1.call-done) | copy-start | bytes 6291460
  149.0 175.6 %all-reduce.13.cloned.1.call-start = ((), (), s32[]{:S(2)}) async-start(), calls=%async_computation.3 | async-start | bytes 196608 | tf_op jit(solution)/shard_map/psum | solution.py:109
  281.2 43.4 %copy-start.6 = (f32[4,24,256]{2,1,0:T(8,128)S(1)}, f32[4,24,256]{2,1,0:T(8,128)}, u32[]{:S(2)}) copy-start(f32[4,24,256]{2,1,0:T(8,128)} %all-reduce.9.cloned.1.call-done) | copy-start | bytes 294916
Sparse Core Ops, SparseCore 0:
  35.7 41.7 all-reduce.8
  108.7 35.2 all-gather.1
  149.1 54.9 all-reduce.10
  283.8 40.8 all-reduce.12
where the time goes:
time: 333 us
  waiting for transfers between devices  155 us (47%)
  other arithmetic  67 us (20%)
  local copies, waits for them, and re-layouts  50.6 us (15%)
  matrix products  22.8 us (7%)
  blocking collectives  16.6 us (5%)
  between operations  16 us (5%)
  starting transfers between devices  4.77 us (1%)
    psum x1, waiting for transfers between devices, per_device(): lax.psum(jnp.sum(prognostic_vector, axis=0), 'mem') / sample_tally_overall  41.8 us
    psum x1, waiting for transfers between devices, per_device(): posterior_adjustment = lax.psum(inc_part, 'mem')  41 us
    psum x1, waiting for transfers between devices, per_device(): gram_matrix, right_side = lax.psum((gram_part, side_part), 'lon')  36.7 us
    all_gather x1, waiting for transfers between devices, per_device(): all_perts = lax.all_gather(obs_perts, 'mem', axis=0, tiled=True)  35.2 us
    another operation x7, other arithmetic, per_device(): factor = jnp.linalg.cholesky(system)  34.6 us
    another operation x4, other arithmetic, per_device(): weights = jax.scipy.linalg.cho_solve((factor, True), right_side)  20 us
    psum x1, blocking collectives, per_device(): gram_matrix, right_side = lax.psum((gram_part, side_part), 'lon')  16.6 us
    dot_general x1, matrix products, per_device(): jnp.einsum('mk,mlij->klij', w_local, sample_departure, precision=lax.Prec...  13.6 us
  transfers between devices with their start and end apart: 6, of which 4 were waited for; matrix products, arithmetic and copies ran while one was open for 6% of the time, Pallas kernels for 0%

commit v1 on v0

--- a/solution.py
+++ b/solution.py
@@ -68,7 +68,10 @@
             flow_lon_ext[:, first_col : first_col + out_cols],
             meridional_wind_padded[:, first_col : first_col + out_cols],
         )
-    sample_centroid = lax.psum(jnp.sum(prognostic_vector, axis=0), "mem") / sample_tally_overall
+    sample_centroid = (
+        jnp.sum(lax.all_gather(jnp.sum(prognostic_vector, axis=0), "mem"), axis=0)
+        / sample_tally_overall
+    )
     sample_departure = prognostic_vector - sample_centroid[None]
     norm_scale = (sample_tally_overall - 1) ** (-0.5)
     obs_slots = obs_index.shape[0]

time: 333 us -> 306 us (0.919)
  waiting for transfers between devices: 155 us -> 111 us
  blocking collectives: 16.6 us -> 27.1 us
  other arithmetic: 67 us -> 72 us
    psum x1 -> x0, waiting for transfers between devices: 41.8 us -> none  [per_device(): lax.psum(jnp.sum(prognostic_vector, axis=0), 'mem') / sample_tally_overall]
    all_gather x0 -> x1, blocking collectives: none -> 10.5 us  [per_device(): lax.all_gather(jnp.sum(prognostic_vector, axis=0), 'mem')]
  transfers between devices with their start and end apart: 6 -> 5, of which waited for: 4 -> 3; matrix products, arithmetic and copies ran while one was open for 6% -> 8% of each run, Pallas kernels for 0% -> 0%
where the time goes in v1:
time: 306 us
  waiting for transfers between devices  111 us (36%)
  other arithmetic  72 us (24%)
  local copies, waits for them, and re-layouts  51.7 us (17%)
  blocking collectives  27.1 us (9%)
  matrix products  22.8 us (7%)
  between operations  16 us (5%)
  starting transfers between devices  4.67 us (2%)
    psum x1, waiting for transfers between devices, per_device(): posterior_adjustment = lax.psum(inc_part, 'mem')  41 us
    psum x1, waiting for transfers between devices, per_device(): gram_matrix, right_side = lax.psum((gram_part, side_part), 'lon')  36.7 us
    another operation x7, other arithmetic, per_device(): factor = jnp.linalg.cholesky(system)  34.6 us
    all_gather x1, waiting for transfers between devices, per_device(): all_perts = lax.all_gather(obs_perts, 'mem', axis=0, tiled=True)  33.7 us
    another operation x4, other arithmetic, per_device(): weights = jax.scipy.linalg.cho_solve((factor, True), right_side)  20 us
    psum x1, blocking collectives, per_device(): gram_matrix, right_side = lax.psum((gram_part, side_part), 'lon')  16.6 us
    dot_general x1, matrix products, per_device(): jnp.einsum('mk,mlij->klij', w_local, sample_departure, precision=lax.Prec...  13.6 us
    gather x1, local copies, waits for them, and re-layouts, per_device(): mean_obs = jnp.take(sample_centroid.reshape(-1), obs_index)  11.8 us
  transfers between devices with their start and end apart: 5, of which 3 were waited for; matrix products, arithmetic and copies ran while one was open for 8% of the time, Pallas kernels for 0%

profile of v1, /device:TPU:0, one launch (start us, length us, event | category | flops | bytes accessed | tf_op | source)
XLA Modules:
  0.0 305.8 jit_solution(1794007520540053138)
XLA Ops:
  7.2 1.8 pad_maximum_fusion.5
  9.0 0.5 collective-permute-start
  9.5 4.1 %collective-permute-start.1 = (f32[40,2,256]{2,1,0:T(2,128)}, f32[40,2,256]{2,1,0:T(2,128)}, u32[]{:S(2)}, u32[]{:S(2)}) collective-permute-start(f32[40,2,256]{2,1,0:T(2,128)} %get-tuple-element.36), channel_id=1, source_target_pairs={{4,0},{8,4},{12,8},{16,12},{20,16},{24,20},{28,24},{0,28},{5,1},{9... | collective-permute-start | bytes 245768 | tf_op jit(solution)/shard_map/ppermute | solution.py:20
  13.6 1.3 compare_and_fusion.1
  14.9 1.3 fusion.30
  16.2 1.6 broadcast_maximum_fusion.2
  18.5 0.8 copy.42
  19.2 5.5 %gather_fusion.1 = f32[2048,2]{1,0:T(8,128)S(1)} fusion(f32[2,4]{0,1:T(4,128)S(1)} %copy.42, s32[2048]{0:T(1024)S(1)} %get-tuple-element.46), kind=kCustom, calls=%fused_computation.1 | custom fusion | bytes 40960 | tf_op jit(solution)/shard_map/jit(_take)/gather | solution.py:83
  25.0 0.9 copy.43
  26.0 2.2 copy.44
  28.1 7.4 %gather_fusion.2 = f32[2048,4]{1,0:T(8,128)S(1)} fusion(f32[4,6144]{0,1:T(8,128)} %bitcast.120, s32[2048]{0:T(1024)S(1)} %get-tuple-element.47), kind=kCustom, calls=%fused_computation.2 | custom fusion | bytes 73728 | tf_op jit(solution)/shard_map/jit(_take)/gather | solution.py:84
  35.6 1.0 select_bitcast_fusion
  36.9 0.7 broadcast_multiply_fusion.1
  37.8 1.1 pad_maximum_fusion
  38.9 0.4 fusion.43
  39.4 0.8 broadcast_maximum_fusion.1
  40.2 0.7 fusion.9
  41.2 0.6 copy-done.6
  41.8 0.5 fusion.39
  42.3 10.5 %all-gather = f32[16,24,256]{2,1,0:T(8,128)S(1)} all-gather(f32[4,24,256]{2,1,0:T(8,128)S(1)} %get-tuple-element.21), channel_id=2, replica_groups=mesh['lon'=8,'mem'=4] {'mem'}, dimensions={0}, use_global_device_ids=true | all-gather | bytes 491520 | tf_op jit(solution)/shard_map/all_gather | solution.py:72
  53.0 6.6 %copy.40 = f32[8,4,24,256]{0,3,2,1:T(8,128)} copy(f32[8,4,24,256]{3,2,1,0:T(8,128)S(1)} %broadcast_subtract_fusion) | data formatting | bytes 1572864 | tf_op jit(solution)/shard_map/sub | solution.py:75
  59.6 11.8 %gather_fusion.3 = f32[2048]{0:T(1024)S(1)} fusion(f32[24576]{0:T(1024)S(1)} %bitcast.113, s32[2048]{0:T(1024)S(1)} %copy-done.8), kind=kCustom, calls=%fused_computation.3 | custom fusion | bytes 24576 | tf_op jit(solution)/shard_map/jit(_take)/gather | solution.py:82
  71.4 10.0 %gather_fusion = f32[2048,8]{1,0:T(8,128)S(1)} fusion(f32[8,24576]{0,1:T(8,128)} %bitcast.114, s32[2048]{0:T(1024)S(1)} %copy-done.8), kind=kCustom, calls=%fused_computation | custom fusion | bytes 139264 | tf_op jit(solution)/shard_map/jit(_take)/gather | solution.py:81
  82.1 0.9 bitcast_multiply_fusion
  83.3 33.7 %all-gather.3.cloned.1.call-done = f32[256,2048]{1,0:T(8,128)} async-done(((f32[64,2048]{1,0:T(8,128)}), f32[256,2048]{1,0:T(8,128)}) %all-gather.3.cloned.1.call-update) | async-done | bytes 2097168 | tf_op jit(solution)/shard_map/all_gather | solution.py:93
  116.9 5.0 %fusion = f32[256,256]{0,1:T(8,128)} fusion(f32[256,2048]{1,0:T(8,128)} %all-gather.3.cloned.1.call-done, f32[2048]{0:T(1024)S(1)} %get-tuple-element.19), kind=kOutput, calls=%fused_computation.6 | convolution fusion | flops 1611137024 | bytes 2367488 | tf_op jit(solution)/shard_map/dot_general | solution.py:94
  122.0 1.7 fusion.44
  123.7 16.6 %psum.22 = f32[256]{0:T(256)S(1)} all-reduce(f32[256]{0:T(256)S(1)} %bitcast.126), channel_id=1, replica_groups=mesh['lon'=8,'mem'=4] {'lon'}, use_global_device_ids=true, to_apply=%region_7.8 | all-reduce | flops 256 | bytes 2048 | tf_op jit(solution)/shard_map/psum | solution.py:96
  140.3 36.7 %all-reduce.8.cloned.1.call-done = f32[256,256]{0,1:T(8,128)} async-done(((f32[256,256]{0,1:T(8,128)}), f32[256,256]{0,1:T(8,128)}) %all-reduce.8.cloned.1.call-update) | async-done | bytes 262160 | tf_op jit(solution)/shard_map/psum | solution.py:96
  177.0 1.0 convert_add_fusion
  178.2 1.0 fusion.19
  179.2 11.7 %cholesky.50 = f32[128,128]{1,0:T(8,128)S(1)} custom-call(f32[128,128]{1,0:T(8,128)S(1)} %cholesky.118), custom_call_target="Cholesky" | custom-call | tf_op jit(solution)/shard_map/jit(cholesky)/cholesky | solution.py:98
  190.9 0.6 compare_reduce_fusion.1
  191.5 9.8 %custom-call.18 = f32[1,128,128]{1,2,0:T(8,128)S(1)} custom-call(f32[1,128,128]{2,1,0:T(8,128)S(1)} %get-tuple-element.44), custom_call_target="InvertDiagBlocksLowerTriangular" | custom-call | tf_op jit(solution)/shard_map/jit(cholesky)/cholesky | solution.py:98
  201.8 11.7 %cholesky.105 = f32[128,128]{1,0:T(8,128)S(1)} custom-call(f32[128,128]{1,0:T(8,128)S(1)} %convolution_subtract_fusion), custom_call_target="Cholesky" | custom-call | tf_op jit(solution)/shard_map/jit(cholesky)/cholesky | solution.py:98
  213.6 0.7 compare_reduce_fusion
  215.6 3.8 %while.1 = (s32[]{:T(128)}, f32[256,256]{1,0:T(8,128)S(1)}, s32[2,2]{1,0:T(2,128)S(1)}, f32[2,128,128]{2,1,0:T(8,128)S(1)}, s32[]{:T(128)}) while((s32[]{:T(128)}, f32[256,256]{1,0:T(8,128)S(1)}, s32[2,2]{1,0:T(2,128)S(1)}, f32[2,128,128]{2,1,0:T(8,128)S(1)}, s32[]{:T(128)}) %tuple.44), condition=%wide.while_cond, body=%wide.while_body.sunk | while | flops 2 | bytes 131189 | solution.py:99
  215.6 0.6 fusion.57
  216.2 1.3 bitcast_dynamic-update-slice_fusion.2
  217.6 0.6 fusion.57
  218.2 1.3 bitcast_dynamic-update-slice_fusion.2
  219.5 19.9 %custom-call.19 = f32[2,128,128]{1,2,0:T(8,128)S(1)} custom-call(f32[2,128,128]{2,1,0:T(8,128)S(1)} %get-tuple-element.9), custom_call_target="InvertDiagBlocksLowerTriangular" | custom-call | tf_op jit(solution)/shard_map/jit(_cho_solve)/triangular_solve | solution.py:99
  240.7 13.6 %fusion.31 = f32[8,4,24,256]{3,0,2,1:T(8,128)S(1)} fusion(f32[8,4,24,256]{0,3,2,1:T(8,128)} %copy.40, f32[32,8]{1,0:T(8,128)S(1)} %reshape.171, s32[]{:T(128)S(6)} %select_n.71), kind=kOutput, calls=%fused_computation.98 | convolution fusion | flops 18874368 | bytes 1576964 | tf_op jit(solution)/shard_map/mk,mlij->klij/dot_general | solution.py:102
  254.5 0.6 multiply_reduce_fusion
  255.2 0.8 fusion.20
  256.0 0.7 bitcast_multiply_fusion.1
  256.7 41.0 %all-reduce.10.cloned.1.call-done = f32[4,24,256]{2,1,0:T(8,128)} async-done(((f32[4,24,256]{2,1,0:T(8,128)}), f32[4,24,256]{2,1,0:T(8,128)}) %all-reduce.10.cloned.1.call-update) | async-done | bytes 98320 | tf_op jit(solution)/shard_map/psum | solution.py:112
  297.7 1.5 fusion.38
  (70 shorter events, 4.6 us)
Async XLA Ops:
  7.2 109.8 %all-gather.3.cloned.1.call-start = ((), (), s32[]{:S(2)}) async-start(), calls=%async_computation | async-start | bytes 2621440 | tf_op jit(solution)/shard_map/all_gather | solution.py:93
  9.0 16.9 %copy-start.5 = (f32[4,24,256]{2,1,0:T(8,128)S(1)}, f32[4,24,256]{2,1,0:T(8,128)}, u32[]{:S(2)}) copy-start(f32[4,24,256]{2,1,0:T(8,128)} %param.13) | copy-start | bytes 294916
  9.0 28.7 %collective-permute-start = (f32[40,2,256]{2,1,0:T(2,128)}, f32[40,2,256]{2,1,0:T(2,128)S(1)}, u32[]{:S(2)}, u32[]{:S(2)}) collective-permute-start(f32[40,2,256]{2,1,0:T(2,128)} %get-tuple-element.35), channel_id=1, source_target_pairs={{0,4},{4,8},{8,12},{12,16},{16,20},{20,24},{24,28},{28,0},{1,5},{5... | collective-permute-start | bytes 245768 | tf_op jit(solution)/shard_map/ppermute | solution.py:17
  9.5 28.2 %collective-permute-start.1 = (f32[40,2,256]{2,1,0:T(2,128)}, f32[40,2,256]{2,1,0:T(2,128)}, u32[]{:S(2)}, u32[]{:S(2)}) collective-permute-start(f32[40,2,256]{2,1,0:T(2,128)} %get-tuple-element.36), channel_id=1, source_target_pairs={{4,0},{8,4},{12,8},{16,12},{20,16},{24,20},{28,24},{0,28},{5,1},{9... | collective-permute-start | bytes 245768 | tf_op jit(solution)/shard_map/ppermute | solution.py:20
  28.1 9.6 %copy-start.1 = (f32[8,4,24,256]{3,2,1,0:T(8,128)S(1)}, f32[8,4,24,256]{3,2,1,0:T(8,128)}, u32[]{:S(2)}) copy-start(f32[8,4,24,256]{3,2,1,0:T(8,128)} %param.9) | copy-start | bytes 2359300
  28.1 9.6 %copy-start.3 = (f32[4,24,256]{2,1,0:T(8,128)S(1)}, f32[4,24,256]{2,1,0:T(8,128)}, u32[]{:S(2)}) copy-start(f32[4,24,256]{2,1,0:T(8,128)} %param.11) | copy-start | bytes 294916
  28.1 9.6 %copy-start.4 = (f32[4,24,256]{2,1,0:T(8,128)S(1)}, f32[4,24,256]{2,1,0:T(8,128)}, u32[]{:S(2)}) copy-start(f32[4,24,256]{2,1,0:T(8,128)} %param.10) | copy-start | bytes 294916
  40.9 0.9 copy-start.6
  42.3 17.3 %copy-start.2 = (f32[8,4,24,256]{3,2,1,0:T(8,128)}, f32[8,4,24,256]{3,2,1,0:T(8,128)S(1)}, u32[]{:S(2)}) copy-start(f32[8,4,24,256]{3,2,1,0:T(8,128)S(1)} %get-tuple-element.22) | copy-start | bytes 2359300
  53.0 6.6 %copy-start.8 = (s32[2048]{0:T(1024)S(1)}, s32[2048]{0:T(1024)}, u32[]{:S(2)}) copy-start(s32[2048]{0:T(1024)} %get-tuple-element.45) | copy-start | bytes 24580
  59.6 21.9 %copy-start.7 = (s32[2048]{0:T(1024)S(1)}, s32[2048]{0:T(1024)}, u32[]{:S(2)}) copy-start(s32[2048]{0:T(1024)} %param.14) | copy-start | bytes 24580
  59.6 21.9 %copy-start.9 = (f32[2048]{0:T(1024)S(1)}, f32[2048]{0:T(1024)}, u32[]{:S(2)}) copy-start(f32[2048]{0:T(1024)} %param.16) | copy-start | bytes 24580
  59.6 21.9 %copy-start.10 = (f32[2048]{0:T(1024)S(1)}, f32[2048]{0:T(1024)}, u32[]{:S(2)}) copy-start(f32[2048]{0:T(1024)} %param.17) | copy-start | bytes 24580
  81.5 1.6 copy-start.11
  83.0 94.0 %all-reduce.8.cloned.1.call-start = ((), (), s32[]{:S(2)}) async-start(), calls=%async_computation.1 | async-start | bytes 524288 | tf_op jit(solution)/shard_map/psum | solution.py:96
  116.9 5.1 %copy-start = (f32[256,2048]{1,0:T(8,128)S(1)}, f32[256,2048]{1,0:T(8,128)}, u32[]{:S(2)}) copy-start(f32[256,2048]{1,0:T(8,128)} %all-gather.3.cloned.1.call-done) | copy-start | bytes 6291460
  121.9 175.8 %all-reduce.10.cloned.1.call-start = ((), (), s32[]{:S(2)}) async-start(), calls=%async_computation.2 | async-start | bytes 196608 | tf_op jit(solution)/shard_map/psum | solution.py:112
Sparse Core Ops, SparseCore 0:
  83.2 33.7 all-gather.2
  122.1 54.9 all-reduce.7
  256.8 40.8 all-reduce.9
